TPU v7x, 32 devices: a whole 2x2x4 slice. The times are simulated.
32 devices in a mesh: grp: 4 (over y, x), tp: 8 (over z, core).
Axes of the slice: x: 2, y: 2, z: 4, core: 2. Of those that a mesh axis runs over, the one named last changes fastest.
Arguments:
- teacher_in: bfloat16 [192, 8192], P('tp', 'grp'), may hold values from -6 to 6
- teacher_gate: bfloat16 [8192, 28672], P('grp', 'tp'), may hold values from -0.0625 to 0.0625
- teacher_up: bfloat16 [8192, 28672], P('grp', 'tp'), may hold values from -0.0625 to 0.0625
- teacher_down: bfloat16 [28672, 8192], P('tp', 'grp'), may hold values from -0.046875 to 0.046875
- student_in: bfloat16 [192, 4096], P('tp', 'grp'), may hold values from -6 to 6
- student_gate: bfloat16 [4096, 14336], P('grp', 'tp'), may hold values from -0.09375 to 0.09375
- student_up: bfloat16 [4096, 14336], P('grp', 'tp'), may hold values from -0.09375 to 0.09375
- student_down: bfloat16 [14336, 4096], P('tp', 'grp'), may hold values from -0.046875 to 0.046875
- projector: bfloat16 [4096, 4, 2048], P('grp', None, 'tp'), may hold values from -0.09375 to 0.09375
Outputs:
- grad_input: float32 [192, 4096], P('tp', 'grp')
- grad_gate: float32 [4096, 14336], P('grp', 'tp')
- grad_up: float32 [4096, 14336], P('grp', 'tp')
- grad_down: float32 [14336, 4096], P('tp', 'grp')
- grad_projector: float32 [4096, 4, 2048], P('grp', None, 'tp')
All inputs are finite; a program needn't handle non-finite values.
Results may differ from a plain program's by a relative error of at most 0.017.
Values may be sent and summed in bfloat16 or wider, within the bound.
No kernel may reach another device: no remote copies, remote signals or barrier semaphores. Data moves between devices by JAX's collectives and lax.ppermute only.
A program may use at most 192 MiB of HBM per device.

v0:
```python
import jax
import jax.numpy as jnp
from jax import lax
from jax.sharding import PartitionSpec as P


def body(
    teacher_in,
    teacher_gate,
    teacher_up,
    teacher_down,
    student_in,
    student_gate,
    student_up,
    student_down,
    projector,
):
    bf = jnp.bfloat16
    fl = jnp.float32
    teacher_pair = jnp.concatenate([teacher_gate, teacher_up], axis=1)
    teacher_width = teacher_gate.shape[1]
    teacher_partial = jnp.dot(
        lax.all_gather(teacher_in, "tp", axis=0, tiled=True),
        teacher_pair,
        preferred_element_type=fl,
    )
    teacher_pre = lax.psum_scatter(teacher_partial, "grp", scatter_dimension=0, tiled=True)
    teacher_hidden = (
        jax.nn.silu(teacher_pre[:, :teacher_width]) * teacher_pre[:, teacher_width:]
    ).astype(bf)
    teacher_sums = jnp.dot(
        lax.all_gather(teacher_hidden, "grp", axis=0, tiled=True),
        teacher_down,
        preferred_element_type=fl,
    )
    teacher_share = lax.psum_scatter(teacher_sums, "tp", scatter_dimension=1, tiled=True)
    teacher_feature = lax.all_to_all(
        teacher_share.astype(bf), "grp", split_axis=0, concat_axis=1, tiled=True
    )
    student_pair = jnp.concatenate([student_gate, student_up], axis=1)
    student_width = student_gate.shape[1]
    input_rows = lax.all_gather(student_in, "tp", axis=0, tiled=True)
    student_partial = jnp.dot(input_rows, student_pair, preferred_element_type=fl)
    student_pre = lax.psum_scatter(student_partial, "grp", scatter_dimension=0, tiled=True)
    gate_values = student_pre[:, :student_width]
    up_values = student_pre[:, student_width:]
    student_hidden = (jax.nn.silu(gate_values) * up_values).astype(bf)
    hidden_rows = lax.all_gather(student_hidden, "grp", axis=0, tiled=True)
    feature_sum = lax.psum(jnp.dot(hidden_rows, student_down, preferred_element_type=fl), "tp")
    student_feature = feature_sum.astype(bf)
    proj_matrix = projector.reshape(projector.shape[0], -1)
    projected = lax.psum_scatter(
        jnp.dot(student_feature, proj_matrix, preferred_element_type=fl),
        "grp",
        scatter_dimension=0,
        tiled=True,
    )
    residual_grad = (projected - teacher_feature.astype(fl)).astype(bf)
    residual_rows = lax.all_gather(residual_grad, "grp", axis=0, tiled=True)
    grad_projector = jnp.dot(student_feature.T, residual_rows, preferred_element_type=fl).reshape(
        projector.shape
    )
    feature_grad = lax.psum(
        jnp.dot(residual_rows, proj_matrix.T, preferred_element_type=fl), "tp"
    ).astype(bf)
    grad_down = jnp.dot(hidden_rows.T, feature_grad, preferred_element_type=fl)
    hidden_grad = lax.psum_scatter(
        jnp.dot(feature_grad, student_down.T, preferred_element_type=fl),
        "grp",
        scatter_dimension=0,
        tiled=True,
    )
    sigmoid_gate = jax.nn.sigmoid(gate_values)
    gate_grad = (
        hidden_grad * up_values * sigmoid_gate * (1.0 + gate_values * (1.0 - sigmoid_gate))
    ).astype(bf)
    up_grad = (hidden_grad * gate_values * sigmoid_gate).astype(bf)
    pair_rows = lax.all_gather(
        jnp.concatenate([gate_grad, up_grad], axis=1), "grp", axis=0, tiled=True
    )
    grad_pair = jnp.dot(input_rows.T, pair_rows, preferred_element_type=fl)
    grad_input = lax.psum_scatter(
        jnp.dot(pair_rows, student_pair.T, preferred_element_type=fl).astype(jnp.bfloat16),
        "tp",
        scatter_dimension=0,
        tiled=True,
    ).astype(jnp.float32)
    return (
        grad_input,
        grad_pair[:, :student_width],
        grad_pair[:, student_width:],
        grad_down,
        grad_projector,
    )


def solution(mesh):
    placed = (
        P("tp", "grp"),
        P("grp", "tp"),
        P("grp", "tp"),
        P("tp", "grp"),
        P("tp", "grp"),
        P("grp", "tp"),
        P("grp", "tp"),
        P("tp", "grp"),
        P("grp", None, "tp"),
    )
    return jax.shard_map(
        body,
        mesh=mesh,
        in_specs=placed,
        out_specs=(
            P("tp", "grp"),
            P("grp", "tp"),
            P("grp", "tp"),
            P("tp", "grp"),
            P("grp", None, "tp"),
        ),
        check_vma=False,
    )
```

profile of v0, /device:TPU:0, one launch (start us, length us, event | category | flops | bytes accessed | tf_op | source)
XLA Modules:
  0.0 422.7 jit_solution(930207206825908747)
XLA Ops:
  7.2 17.4 %all_gather.20 = bf16[192,2048]{1,0:T(8,128)(2,1)S(1)} all-gather(bf16[24,2048]{1,0:T(8,128)(2,1)} %param.9), channel_id=1, replica_groups=mesh['grp'=4,'tp'=8] {'tp'}, dimensions={0}, use_global_device_ids=true | all-gather | bytes 884736 | tf_op jit(solution)/shard_map/all_gather | solution.py:23
  24.6 14.3 %fusion.4 = f32[192,7168]{1,0:T(8,128)} fusion(bf16[192,2048]{1,0:T(8,128)(2,1)S(1)} %all_gather.20, bf16[2048,3584]{1,0:T(8,128)(2,1)} %param.11, bf16[2048,3584]{1,0:T(8,128)(2,1)} %param.10), kind=kOutput, calls=%fused_computation.4 | convolution fusion | flops 5695864832 | bytes 35651584 | tf_op jit(solution)/shard_map/dot_general | solution.py:22
  39.0 64.8 %reduce-scatter.11.cloned.1.call-done = f32[48,7168]{1,0:T(8,128)} async-done(((f32[192,7168]{1,0:T(8,128)}), f32[48,7168]{1,0:T(8,128)}) %reduce-scatter.11.cloned.1.call-update) | async-done | bytes 1376272 | tf_op jit(solution)/shard_map/reduce_scatter | solution.py:27
  103.8 2.2 fusion.7
  106.1 14.6 %all_gather.18 = bf16[192,1024]{1,0:T(8,128)(2,1)S(1)} all-gather(bf16[24,1024]{1,0:T(8,128)(2,1)S(1)} %copy-done.8), channel_id=1, replica_groups=mesh['grp'=4,'tp'=8] {'tp'}, dimensions={0}, use_global_device_ids=true | all-gather | bytes 442368 | tf_op jit(solution)/shard_map/all_gather | solution.py:42
  120.7 2.5 constant_dynamic-update-slice_fusion.1
  123.5 3.0 copy-done
  126.6 3.1 convolution_bitcast_fusion.1
  129.8 5.7 %all-gather.3.cloned.1.call-done = bf16[192,3584]{1,0:T(8,128)(2,1)} async-done(((bf16[48,3584]{1,0:T(8,128)(2,1)}), bf16[192,3584]{1,0:T(8,128)(2,1)}) %all-gather.3.cloned.1.call-update) | async-done | bytes 1376272 | tf_op jit(solution)/shard_map/all_gather | solution.py:32
  135.4 9.8 %fusion.19 = f32[192,2048]{1,0:T(8,128)} fusion(bf16[192,3584]{1,0:T(8,128)(2,1)} %all-gather.3.cloned.1.call-done, bf16[3584,2048]{1,0:T(8,128)(2,1)} %param.12), kind=kOutput, calls=%fused_computation.30 | convolution fusion | flops 2818572288 | bytes 17629184 | tf_op jit(solution)/shard_map/dot_general | solution.py:31
  145.3 2.2 copy.23
  147.4 32.3 %reduce-scatter.7.cloned.1.call-done = f32[48,3584]{1,0:T(8,128)} async-done(((f32[192,3584]{1,0:T(8,128)}), f32[48,3584]{1,0:T(8,128)}) %reduce-scatter.7.cloned.1.call-update) | async-done | bytes 688144 | tf_op jit(solution)/shard_map/reduce_scatter | solution.py:44
  180.9 10.7 %all_gather.19 = bf16[192,1792]{1,0:T(8,128)(2,1)S(1)} all-gather(bf16[48,1792]{1,0:T(8,128)(2,1)S(1)} %multiply_convert_fusion.2), channel_id=1, replica_groups=mesh['grp'=4,'tp'=8] {'grp'}, dimensions={0}, use_global_device_ids=true | all-gather | bytes 860160 | tf_op jit(solution)/shard_map/all_gather | solution.py:48
  191.6 3.8 fusion.18
  195.4 38.1 %all-reduce.2 = bf16[192,1024]{1,0:T(8,128)(2,1)S(1)} all-reduce(f32[192,1024]{1,0:T(8,128)} %fusion.18), channel_id=1, replica_groups=mesh['grp'=4,'tp'=8] {'tp'}, use_global_device_ids=true, to_apply=%region_1.2 | all-reduce | flops 196608 | bytes 1179648 | tf_op jit(solution)/shard_map/psum | solution.py:49
  233.5 1.5 fusion.24
  236.1 7.8 %all_to_all.13 = bf16[4,48,256]{2,1,0:T(8,128)(2,1)S(1)} all-to-all(bf16[4,48,256]{2,1,0:T(8,128)(2,1)S(1)} %bitcast.40), channel_id=1, replica_groups=mesh['grp'=4,'tp'=8] {'grp'}, dimensions={0} | all-to-all | bytes 196608 | tf_op jit(solution)/shard_map/all_to_all | solution.py:37
  243.9 14.5 %reduce-scatter.9.cloned.1.call-done = f32[48,1024]{1,0:T(8,128)} async-done(((f32[192,1024]{1,0:T(8,128)}), f32[48,1024]{1,0:T(8,128)}) %reduce-scatter.9.cloned.1.call-update) | async-done | bytes 196624 | tf_op jit(solution)/shard_map/reduce_scatter | solution.py:52
  259.4 9.6 %all_gather.22 = bf16[192,1024]{1,0:T(8,128)(2,1)S(1)} all-gather(bf16[48,1024]{1,0:T(8,128)(2,1)S(1)} %subtract_convert_fusion), channel_id=1, replica_groups=mesh['grp'=4,'tp'=8] {'grp'}, dimensions={0}, use_global_device_ids=true | all-gather | bytes 491520 | tf_op jit(solution)/shard_map/all_gather | solution.py:59
  269.7 1.7 fusion.20
  271.4 35.0 %all-reduce.3 = bf16[192,1024]{1,0:T(8,128)(2,1)S(1)} all-reduce(f32[192,1024]{1,0:T(8,128)} %fusion.20), channel_id=1, replica_groups=mesh['grp'=4,'tp'=8] {'tp'}, use_global_device_ids=true, to_apply=%region_5.6 | all-reduce | flops 196608 | bytes 1179648 | tf_op jit(solution)/shard_map/psum | solution.py:63
  306.4 4.5 %fusion.22 = f32[192,1792]{1,0:T(8,128)} fusion(bf16[192,1024]{1,0:T(8,128)(2,1)S(1)} %all-reduce.3, bf16[1792,1024]{1,0:T(8,128)(2,1)} %param.16), kind=kOutput, calls=%fused_computation.33 | convolution fusion | flops 704643072 | bytes 5439488 | tf_op jit(solution)/shard_map/dot_general | solution.py:68
  311.1 27.0 %reduce-scatter.15.cloned.1.call-done = f32[48,1792]{1,0:T(8,128)} async-done(((f32[192,1792]{1,0:T(8,128)}), f32[48,1792]{1,0:T(8,128)}) %reduce-scatter.15.cloned.1.call-update) | async-done | bytes 344080 | tf_op jit(solution)/shard_map/reduce_scatter | solution.py:67
  340.1 2.8 fusion.23
  342.9 5.3 %copy.21 = f32[1024,4,256]{2,1,0:T(4,128)} copy(f32[1024,4,256]{0,2,1:T(8,128)} %bitcast.35) | data formatting | bytes 8388608
  348.2 4.2 fusion.21
  352.4 17.1 %all-gather.5.cloned.1.call-done = bf16[192,3584]{1,0:T(8,128)(2,1)} async-done(((bf16[48,3584]{1,0:T(8,128)(2,1)}), bf16[192,3584]{1,0:T(8,128)(2,1)}) %all-gather.5.cloned.1.call-update) | async-done | bytes 1376272 | tf_op jit(solution)/shard_map/all_gather | solution.py:78
  369.4 6.9 %convolution_convert_fusion = bf16[192,1024]{1,0:T(8,128)(2,1)} fusion(bf16[192,3584]{1,0:T(8,128)(2,1)} %all-gather.5.cloned.1.call-done, bf16[1024,3584]{1,0:T(8,128)(2,1)} %copy-done), kind=kOutput, calls=%fused_computation.7 | convolution fusion | flops 1409482752 | bytes 9109504 | tf_op jit(solution)/shard_map/dot_general | solution.py:83
  376.4 7.3 %convolution_bitcast_fusion = f32[1024,3584]{0,1:T(8,128)} fusion(bf16[192,3584]{1,0:T(8,128)(2,1)S(1)} %copy-done.7, bf16[192,1024]{1,0:T(8,128)(2,1)S(1)} %copy-done.2), kind=kOutput, calls=%fused_computation.5 | convolution fusion | flops 1409286144 | bytes 16449536 | tf_op jit(solution)/shard_map/dot_general | solution.py:81
  383.7 13.9 %fusion.17 = (f32[1024,1792]{0,1:T(8,128)}, f32[1024,1792]{0,1:T(8,128)}) fusion(f32[1024,3584]{0,1:T(8,128)} %convolution_bitcast_fusion), kind=kLoop, calls=%fused_computation.28 | loop fusion | bytes 29360128 | tf_op jit(solution)/shard_map/slice | solution.py:91
  397.6 8.4 %copy.19 = f32[1024,1792]{1,0:T(8,128)} copy(f32[1024,1792]{0,1:T(8,128)} %get-tuple-element.16) | data formatting | bytes 14680064
  406.0 8.4 %copy.20 = f32[1024,1792]{1,0:T(8,128)} copy(f32[1024,1792]{0,1:T(8,128)} %get-tuple-element.15) | data formatting | bytes 14680064
  (44 shorter events, 8.2 us)
Async XLA Ops:
  7.2 96.6 %reduce-scatter.11.cloned.1.call-start = ((), (), s32[]{:S(2)}) async-start(), calls=%async_computation.9 | async-start | bytes 6881280 | tf_op jit(solution)/shard_map/reduce_scatter | solution.py:27
  38.9 67.1 %copy-start.8 = (bf16[24,1024]{1,0:T(8,128)(2,1)S(1)}, bf16[24,1024]{1,0:T(8,128)(2,1)}, u32[]{:S(2)}) copy-start(bf16[24,1024]{1,0:T(8,128)(2,1)} %param.13) | copy-start | bytes 147460
  39.0 96.5 %all-gather.3.cloned.1.call-start = ((), (), s32[]{:S(2)}) async-start(), calls=%async_computation.10 | async-start | bytes 1720320 | tf_op jit(solution)/shard_map/all_gather | solution.py:32
  106.0 73.7 %reduce-scatter.7.cloned.1.call-start = ((), (), s32[]{:S(2)}) async-start(), calls=%async_computation.7 | async-start | bytes 3440640 | tf_op jit(solution)/shard_map/reduce_scatter | solution.py:44
  106.1 17.1 %copy-start.3 = (bf16[1024,1792]{1,0:T(8,128)(2,1)S(1)}, bf16[1024,1792]{1,0:T(8,128)(2,1)}, u32[]{:S(2)}) copy-start(bf16[1024,1792]{1,0:T(8,128)(2,1)} %param.15) | copy-start | bytes 11010052
  120.7 2.8 copy-start.1
  123.5 3.1 copy-start
  129.7 105.4 %reduce-scatter.13.cloned.1.call-start = ((), (), s32[]{:S(2)}) async-start(), calls=%async_computation.11 | async-start | bytes 1769472 | tf_op jit(solution)/shard_map/reduce_scatter | solution.py:36
  145.2 113.2 %reduce-scatter.9.cloned.1.call-start = ((), (), s32[]{:S(2)}) async-start(), calls=%async_computation.8 | async-start | bytes 983040 | tf_op jit(solution)/shard_map/reduce_scatter | solution.py:52
  235.0 103.1 %reduce-scatter.15.cloned.1.call-start = ((), (), s32[]{:S(2)}) async-start(), calls=%async_computation.12 | async-start | bytes 1720320 | tf_op jit(solution)/shard_map/reduce_scatter | solution.py:67
  268.9 0.7 copy-start.4
  271.4 66.8 %copy-start.6 = (f32[48,3584]{1,0:T(8,128)S(1)}, f32[48,3584]{1,0:T(8,128)}, u32[]{:S(2)}) copy-start(f32[48,3584]{1,0:T(8,128)} %reduce-scatter.7.cloned.1.call-done) | copy-start | bytes 2064388
  271.4 68.7 %copy-start.5 = (bf16[192,1024]{1,0:T(8,128)(2,1)S(1)}, bf16[192,1024]{1,0:T(8,128)(2,1)}, u32[]{:S(2)}) copy-start(bf16[192,1024]{1,0:T(8,128)(2,1)} %copy-done.4) | copy-start | bytes 1179652
  310.9 58.5 %all-gather.5.cloned.1.call-start = ((), (), s32[]{:S(2)}) async-start(), calls=%async_computation.13 | async-start | bytes 1720320 | tf_op jit(solution)/shard_map/all_gather | solution.py:78
  340.1 74.3 %reduce-scatter.17.cloned.1.call-start = ((), (), s32[]{:S(2)}) async-start(), calls=%async_computation.14 | async-start | bytes 442368 | tf_op jit(solution)/shard_map/reduce_scatter | solution.py:82
  352.4 24.0 %copy-start.2 = (bf16[192,1024]{1,0:T(8,128)(2,1)S(1)}, bf16[192,1024]{1,0:T(8,128)(2,1)}, u32[]{:S(2)}) copy-start(bf16[192,1024]{1,0:T(8,128)(2,1)} %copy-done.1) | copy-start | bytes 1179652
  369.4 6.9 %copy-start.7 = (bf16[192,3584]{1,0:T(8,128)(2,1)S(1)}, bf16[192,3584]{1,0:T(8,128)(2,1)}, u32[]{:S(2)}) copy-start(bf16[192,3584]{1,0:T(8,128)(2,1)} %all-gather.5.cloned.1.call-done) | copy-start | bytes 4128772
Sparse Core Ops, SparseCore 0:
  39.1 64.6 reduce-scatter.10
  106.2 29.1 all-gather.2
  139.0 40.6 reduce-scatter.6
  182.4 36.0 reduce-scatter.12
  235.2 23.2 reduce-scatter.8
  311.0 27.0 reduce-scatter.14
  340.2 29.1 all-gather.4
  376.5 31.1 reduce-scatter.16
where the time goes:
time: 424 us; the launch traced here: 423 us
  waiting for transfers between devices  161 us (38%)
  blocking collectives  133 us (31%)
  matrix products  59.9 us (14%)
  local copies, waits for them, and re-layouts  44.7 us (11%)
  between operations  14.3 us (3%)
  other arithmetic  8.64 us (2%)
    reduce_scatter x1, waiting for transfers between devices, body(): lax.psum_scatter(teacher_partial, 'grp', scatter_dimension=0, tiled=True)  64.8 us
    psum x1, blocking collectives, body(): lax.psum(jnp.dot(hidden_rows, student_down, preferred_element_type=fl), '...  38.1 us
    psum x1, blocking collectives, body(): lax.psum(jnp.dot(residual_rows, proj_matrix.T, preferred_element_type=fl)...  35 us
    reduce_scatter x1, waiting for transfers between devices, body(): lax.psum_scatter(student_partial, 'grp', scatter_dimension=0, tiled=True)  32.3 us
    unnamed x23, local copies, waits for them, and re-layouts  30.4 us
    reduce_scatter x1, waiting for transfers between devices, body(): lax.psum_scatter(jnp.dot(feature_grad, student_down.T, preferred_element_...  27 us
    all_gather x1, blocking collectives, body(): lax.all_gather(teacher_in, 'tp', axis=0, tiled=True)  17.4 us
    all_gather x1, waiting for transfers between devices, body(): lax.all_gather(jnp.concatenate([gate_grad, up_grad], axis=1), 'grp', axis...  17.1 us
  transfers between devices with their start and end apart: 8, of which 6 were waited for; matrix products, arithmetic and copies ran while one was open for 18% of the time, Pallas kernels for 0%

commit v1 on v0

--- a/solution.py
+++ b/solution.py
@@ -39,7 +39,23 @@
     )
     student_pair = jnp.concatenate([student_gate, student_up], axis=1)
     student_width = student_gate.shape[1]
-    input_rows = lax.all_gather(student_in, "tp", axis=0, tiled=True)
+    far_arr = lax.axis_size("tp")
+    later = lax.axis_index("tp")
+    view_out, r_now, block_now = (far_arr, later, student_in.shape[0])
+    sides = [m * view_out if jj == 0 else m for jj, m in enumerate(student_in.shape)]
+    x_new = jnp.zeros(sides, student_in.dtype)
+    input_rows = lax.dynamic_update_slice_in_dim(x_new, student_in, r_now * block_now, axis=0)
+    then = y1 = student_in
+    for p in range(1, view_out // 2 + 1):
+        then = lax.ppermute(then, "tp", [(jj, (jj + 1) % view_out) for jj in range(view_out)])
+        input_rows = lax.dynamic_update_slice_in_dim(
+            input_rows, then, (r_now - p) % view_out * block_now, axis=0
+        )
+        if 2 * p < view_out:
+            y1 = lax.ppermute(y1, "tp", [(jj, (jj - 1) % view_out) for jj in range(view_out)])
+            input_rows = lax.dynamic_update_slice_in_dim(
+                input_rows, y1, (r_now + p) % view_out * block_now, axis=0
+            )
     student_partial = jnp.dot(input_rows, student_pair, preferred_element_type=fl)
     student_pre = lax.psum_scatter(student_partial, "grp", scatter_dimension=0, tiled=True)
     gate_values = student_pre[:, :student_width]

time: 424 us -> 417 us (0.983)
  local copies, waits for them, and re-layouts: 44.7 us -> 27 us
  blocking collectives: 133 us -> 119 us
  waiting for transfers between devices: 161 us -> 173 us
  starting transfers between devices: 0.51 us -> 11 us
    unnamed x23 -> x19, local copies, waits for them, and re-layouts: 30.4 us -> 13.2 us
    all_gather x1 -> x0, blocking collectives: 14.6 us -> none  [body(): input_rows = lax.all_gather(student_in, 'tp', axis=0, tiled=True)]
    reduce_scatter x1, waiting for transfers between devices: 0.01 us -> 12.3 us  [body(): lax.psum_scatter(jnp.dot(pair_rows, student_pair.T, preferred_element_typ...]
    ppermute x0 -> x7, starting transfers between devices: none -> 10.7 us  [the longest x3 10.3 us: body(): lax.ppermute(y1, 'tp', [(jj, (jj - 1) % view_out) for jj in range(view_ou...]
    ppermute x0 -> x7, waiting for transfers between devices: none -> 9.05 us  [the longest x4 9.05 us: body(): lax.ppermute(then, 'tp', [(jj, (jj + 1) % view_out) for jj in range(view_...]
    all_gather x1, waiting for transfers between devices: 5.65 us -> 0.08 us  [body(): lax.all_gather(teacher_hidden, 'grp', axis=0, tiled=True)]
    reduce_scatter x1, waiting for transfers between devices: 64.8 us -> 60.5 us  [body(): lax.psum_scatter(teacher_partial, 'grp', scatter_dimension=0, tiled=True)]
  transfers between devices with their start and end apart: 8 -> 15, of which waited for: 6 -> 10; matrix products, arithmetic and copies ran while one was open for 18% -> 16% of each run, Pallas kernels for 0% -> 0%
where the time goes in v1:
time: 417 us; the launch traced here: 416 us
  waiting for transfers between devices  173 us (41%)
  blocking collectives  119 us (29%)
  matrix products  63.1 us (15%)
  local copies, waits for them, and re-layouts  27 us (6%)
  between operations  14.5 us (3%)
  starting transfers between devices  11 us (3%)
  other arithmetic  8.64 us (2%)
    reduce_scatter x1, waiting for transfers between devices, body(): lax.psum_scatter(teacher_partial, 'grp', scatter_dimension=0, tiled=True)  60.5 us
    psum x1, blocking collectives, body(): lax.psum(jnp.dot(hidden_rows, student_down, preferred_element_type=fl), '...  38.1 us
    psum x1, blocking collectives, body(): lax.psum(jnp.dot(residual_rows, proj_matrix.T, preferred_element_type=fl)...  35.1 us
    reduce_scatter x1, waiting for transfers between devices, body(): lax.psum_scatter(student_partial, 'grp', scatter_dimension=0, tiled=True)  32.3 us
    reduce_scatter x1, waiting for transfers between devices, body(): lax.psum_scatter(jnp.dot(feature_grad, student_down.T, preferred_element_...  27.2 us
    all_gather x1, blocking collectives, body(): lax.all_gather(teacher_in, 'tp', axis=0, tiled=True)  17.4 us
    all_gather x1, waiting for transfers between devices, body(): lax.all_gather(jnp.concatenate([gate_grad, up_grad], axis=1), 'grp', axis...  17.1 us
    reduce_scatter x1, waiting for transfers between devices, body(): lax.psum_scatter(jnp.dot(student_feature, proj_matrix, preferred_element_...  14.6 us
  transfers between devices with their start and end apart: 15, of which 10 were waited for; matrix products, arithmetic and copies ran while one was open for 16% of the time, Pallas kernels for 0%

profile of v1, /device:TPU:0, one launch (start us, length us, event | category | flops | bytes accessed | tf_op | source)
XLA Modules:
  0.0 416.3 jit_solution(6634452417784411079)
XLA Ops:
  7.2 17.4 %all_gather.16 = bf16[192,2048]{1,0:T(8,128)(2,1)S(1)} all-gather(bf16[24,2048]{1,0:T(8,128)(2,1)} %param.9), channel_id=1, replica_groups=mesh['grp'=4,'tp'=8] {'tp'}, dimensions={0}, use_global_device_ids=true | all-gather | bytes 884736 | tf_op jit(solution)/shard_map/all_gather | solution.py:23
  24.6 14.3 %fusion.4 = f32[192,7168]{1,0:T(8,128)} fusion(bf16[192,2048]{1,0:T(8,128)(2,1)S(1)} %all_gather.16, bf16[2048,3584]{1,0:T(8,128)(2,1)} %param.11, bf16[2048,3584]{1,0:T(8,128)(2,1)} %param.10), kind=kOutput, calls=%fused_computation.4 | convolution fusion | flops 5695864832 | bytes 35651584 | tf_op jit(solution)/shard_map/dot_general | solution.py:22
  40.1 3.2 collective-permute-start.1
  43.3 60.5 %reduce-scatter.11.cloned.1.call-done = f32[48,7168]{1,0:T(8,128)} async-done(((f32[192,7168]{1,0:T(8,128)}), f32[48,7168]{1,0:T(8,128)}) %reduce-scatter.11.cloned.1.call-update) | async-done | bytes 1376272 | tf_op jit(solution)/shard_map/reduce_scatter | solution.py:27
  103.8 2.2 fusion.7
  106.1 4.3 %constant_dynamic-update-slice_fusion.1 = bf16[1024,3584]{1,0:T(8,128)(2,1)} fusion(bf16[1024,1792]{1,0:T(8,128)(2,1)} %param.14), kind=kLoop, calls=%fused_computation.24 | loop fusion | bytes 7340032
  110.4 2.1 constant_dynamic-update-slice_fusion
  112.7 3.5 collective-permute-start.3
  118.1 3.5 collective-permute-start.5
  121.7 1.9 collective-permute-done.4
  123.6 5.3 %collective-permute-done.6 = bf16[24,1024]{1,0:T(8,128)(2,1)S(1)} collective-permute-done((bf16[24,1024]{1,0:T(8,128)(2,1)S(1)}, bf16[24,1024]{1,0:T(8,128)(2,1)S(1)}, u32[]{:S(2)}, u32[]{:S(2)}) %collective-permute-start.6) | collective-permute-done | bytes 49184 | tf_op jit(solution)/shard_map/ppermute | solution.py:50
  128.9 6.4 %fusion.18 = f32[192,3584]{1,0:T(8,128)} fusion(bf16[192,1024]{1,0:T(8,128)(2,1)S(1)} %constant_dynamic-update-slice_fusion.2, bf16[1024,3584]{1,0:T(8,128)(2,1)} %constant_dynamic-update-slice_fusion), kind=kOutput, calls=%fused_computation.35 | convolution fusion | flops 1409286144 | bytes 10485760 | tf_op jit(solution)/shard_map/dot_general | solution.py:59
  135.4 9.8 %fusion.20 = f32[192,2048]{1,0:T(8,128)} fusion(bf16[192,3584]{1,0:T(8,128)(2,1)} %all-gather.3.cloned.1.call-done, bf16[3584,2048]{1,0:T(8,128)(2,1)} %param.12), kind=kOutput, calls=%fused_computation.37 | convolution fusion | flops 2818572288 | bytes 17629184 | tf_op jit(solution)/shard_map/dot_general | solution.py:31
  145.3 2.2 copy.19
  147.4 32.3 %reduce-scatter.7.cloned.1.call-done = f32[48,3584]{1,0:T(8,128)} async-done(((f32[192,3584]{1,0:T(8,128)}), f32[48,3584]{1,0:T(8,128)}) %reduce-scatter.7.cloned.1.call-update) | async-done | bytes 688144 | tf_op jit(solution)/shard_map/reduce_scatter | solution.py:60
  180.9 10.7 %all_gather.15 = bf16[192,1792]{1,0:T(8,128)(2,1)S(1)} all-gather(bf16[48,1792]{1,0:T(8,128)(2,1)S(1)} %multiply_convert_fusion.2), channel_id=1, replica_groups=mesh['grp'=4,'tp'=8] {'grp'}, dimensions={0}, use_global_device_ids=true | all-gather | bytes 860160 | tf_op jit(solution)/shard_map/all_gather | solution.py:64
  191.6 3.8 fusion.19
  195.4 38.1 %all-reduce.2 = bf16[192,1024]{1,0:T(8,128)(2,1)S(1)} all-reduce(f32[192,1024]{1,0:T(8,128)} %fusion.19), channel_id=1, replica_groups=mesh['grp'=4,'tp'=8] {'tp'}, use_global_device_ids=true, to_apply=%region_1.2 | all-reduce | flops 196608 | bytes 1179648 | tf_op jit(solution)/shard_map/psum | solution.py:65
  236.1 7.9 %all_to_all.13 = bf16[4,48,256]{2,1,0:T(8,128)(2,1)S(1)} all-to-all(bf16[4,48,256]{2,1,0:T(8,128)(2,1)S(1)} %bitcast.36), channel_id=1, replica_groups=mesh['grp'=4,'tp'=8] {'grp'}, dimensions={0} | all-to-all | bytes 196608 | tf_op jit(solution)/shard_map/all_to_all | solution.py:37
  244.0 14.6 %reduce-scatter.9.cloned.1.call-done = f32[48,1024]{1,0:T(8,128)} async-done(((f32[192,1024]{1,0:T(8,128)}), f32[48,1024]{1,0:T(8,128)}) %reduce-scatter.9.cloned.1.call-update) | async-done | bytes 196624 | tf_op jit(solution)/shard_map/reduce_scatter | solution.py:68
  259.6 9.6 %all_gather.18 = bf16[192,1024]{1,0:T(8,128)(2,1)S(1)} all-gather(bf16[48,1024]{1,0:T(8,128)(2,1)S(1)} %subtract_convert_fusion), channel_id=1, replica_groups=mesh['grp'=4,'tp'=8] {'grp'}, dimensions={0}, use_global_device_ids=true | all-gather | bytes 491520 | tf_op jit(solution)/shard_map/all_gather | solution.py:75
  271.7 35.1 %all-reduce.3 = bf16[192,1024]{1,0:T(8,128)(2,1)S(1)} all-reduce(f32[192,1024]{1,0:T(8,128)} %fusion.21), channel_id=1, replica_groups=mesh['grp'=4,'tp'=8] {'tp'}, use_global_device_ids=true, to_apply=%region_5.6 | all-reduce | flops 196608 | bytes 1179648 | tf_op jit(solution)/shard_map/psum | solution.py:79
  306.7 4.5 %fusion.24 = f32[192,1792]{1,0:T(8,128)} fusion(bf16[192,1024]{1,0:T(8,128)(2,1)S(1)} %all-reduce.3, bf16[1792,1024]{1,0:T(8,128)(2,1)} %param.16), kind=kOutput, calls=%fused_computation.41 | convolution fusion | flops 704643072 | bytes 5439488 | tf_op jit(solution)/shard_map/dot_general | solution.py:84
  311.3 27.2 %reduce-scatter.15.cloned.1.call-done = f32[48,1792]{1,0:T(8,128)} async-done(((f32[192,1792]{1,0:T(8,128)}), f32[48,1792]{1,0:T(8,128)}) %reduce-scatter.15.cloned.1.call-update) | async-done | bytes 344080 | tf_op jit(solution)/shard_map/reduce_scatter | solution.py:83
  340.6 2.8 fusion.25
  343.3 5.3 %copy.17 = f32[1024,4,256]{2,1,0:T(4,128)} copy(f32[1024,4,256]{0,2,1:T(8,128)} %bitcast.31) | data formatting | bytes 8388608
  348.6 4.2 %fusion.23 = f32[1792,1024]{1,0:T(8,128)} fusion(bf16[192,1792]{1,0:T(8,128)(2,1)S(1)} %all_gather.15, bf16[192,1024]{1,0:T(8,128)(2,1)S(1)} %all-reduce.3), kind=kOutput, calls=%fused_computation.40 | convolution fusion | flops 704643072 | bytes 8421376 | tf_op jit(solution)/shard_map/dot_general | solution.py:82
  352.8 17.1 %all-gather.5.cloned.1.call-done = bf16[192,3584]{1,0:T(8,128)(2,1)} async-done(((bf16[48,3584]{1,0:T(8,128)(2,1)}), bf16[192,3584]{1,0:T(8,128)(2,1)}) %all-gather.5.cloned.1.call-update) | async-done | bytes 1376272 | tf_op jit(solution)/shard_map/all_gather | solution.py:94
  369.9 6.9 %convolution_convert_fusion = bf16[192,1024]{1,0:T(8,128)(2,1)} fusion(bf16[192,3584]{1,0:T(8,128)(2,1)} %all-gather.5.cloned.1.call-done, bf16[1024,3584]{1,0:T(8,128)(2,1)} %constant_dynamic-update-slice_fusion), kind=kOutput, calls=%fused_computation.5 | convolution fusion | flops 1409482752 | bytes 9109504 | tf_op jit(solution)/shard_map/dot_general | solution.py:99
  376.8 7.3 %fusion.22 = f32[1024,3584]{1,0:T(8,128)} fusion(bf16[192,1024]{1,0:T(8,128)(2,1)S(1)} %copy-done.1, bf16[192,3584]{1,0:T(8,128)(2,1)S(1)} %copy-done.6), kind=kOutput, calls=%fused_computation.39 | convolution fusion | flops 1409286144 | bytes 16449536 | tf_op jit(solution)/shard_map/dot_general | solution.py:97
  384.1 11.6 %fusion.17 = (f32[1024,1792]{1,0:T(8,128)}, f32[1024,1792]{1,0:T(8,128)}) fusion(f32[1024,3584]{1,0:T(8,128)} %fusion.22), kind=kLoop, calls=%fused_computation.34 | loop fusion | bytes 29360128 | tf_op jit(solution)/shard_map/slice | solution.py:107
  395.7 12.3 %reduce-scatter.17.cloned.1.call-done = bf16[24,1024]{1,0:T(8,128)(2,1)} async-done(((bf16[192,1024]{1,0:T(8,128)(2,1)}), bf16[24,1024]{1,0:T(8,128)(2,1)}) %reduce-scatter.17.cloned.1.call-update) | async-done | bytes 49168 | tf_op jit(solution)/shard_map/reduce_scatter | solution.py:98
  (62 shorter events, 14.1 us)
Async XLA Ops:
  7.2 96.6 %reduce-scatter.11.cloned.1.call-start = ((), (), s32[]{:S(2)}) async-start(), calls=%async_computation.9 | async-start | bytes 6881280 | tf_op jit(solution)/shard_map/reduce_scatter | solution.py:27
  38.9 0.8 copy-start.7
  39.0 96.5 %all-gather.3.cloned.1.call-start = ((), (), s32[]{:S(2)}) async-start(), calls=%async_computation.10 | async-start | bytes 1720320 | tf_op jit(solution)/shard_map/all_gather | solution.py:32
  39.7 72.9 %collective-permute-start = (bf16[24,1024]{1,0:T(8,128)(2,1)S(1)}, bf16[24,1024]{1,0:T(8,128)(2,1)S(1)}, u32[]{:S(2)}, u32[]{:S(2)}) collective-permute-start(bf16[24,1024]{1,0:T(8,128)(2,1)S(1)} %copy-done.7), channel_id=1, source_target_pairs={{0,1},{1,2},{2,3},{3,4},{4,5},{5,6},{6,7},{7,0},{8,9},{9,10},{10,1... | collective-permute-start | bytes 147464 | tf_op jit(solution)/shard_map/ppermute | solution.py:50
  40.1 72.6 %collective-permute-start.1 = (bf16[24,1024]{1,0:T(8,128)(2,1)S(1)}, bf16[24,1024]{1,0:T(8,128)(2,1)S(1)}, u32[]{:S(2)}, u32[]{:S(2)}) collective-permute-start(bf16[24,1024]{1,0:T(8,128)(2,1)S(1)} %copy-done.7), channel_id=1, source_target_pairs={{0,7},{1,0},{2,1},{3,2},{4,3},{5,4},{6,5},{7,6},{8,15},{9,8},{10,9... | collective-permute-start | bytes 147464 | tf_op jit(solution)/shard_map/ppermute | solution.py:55
  106.0 73.7 %reduce-scatter.7.cloned.1.call-start = ((), (), s32[]{:S(2)}) async-start(), calls=%async_computation.7 | async-start | bytes 3440640 | tf_op jit(solution)/shard_map/reduce_scatter | solution.py:60
  106.1 4.3 %copy-start.2 = (bf16[1024,1792]{1,0:T(8,128)(2,1)S(1)}, bf16[1024,1792]{1,0:T(8,128)(2,1)}, u32[]{:S(2)}) copy-start(bf16[1024,1792]{1,0:T(8,128)(2,1)} %param.15) | copy-start | bytes 11010052
  112.6 5.5 %collective-permute-start.2 = (bf16[24,1024]{1,0:T(8,128)(2,1)S(1)}, bf16[24,1024]{1,0:T(8,128)(2,1)S(1)}, u32[]{:S(2)}, u32[]{:S(2)}) collective-permute-start(bf16[24,1024]{1,0:T(8,128)(2,1)S(1)} %collective-permute-done), channel_id=1, source_target_pairs={{0,1},{1,2},{2,3},{3,4},{4,5},{5,6},{6,7},{7,0},{8,9},{9,10},{10,1... | collective-permute-start | bytes 147464 | tf_op jit(solution)/shard_map/ppermute | solution.py:50
  112.7 5.4 %collective-permute-start.3 = (bf16[24,1024]{1,0:T(8,128)(2,1)S(1)}, bf16[24,1024]{1,0:T(8,128)(2,1)S(1)}, u32[]{:S(2)}, u32[]{:S(2)}) collective-permute-start(bf16[24,1024]{1,0:T(8,128)(2,1)S(1)} %collective-permute-done.1), channel_id=1, source_target_pairs={{0,7},{1,0},{2,1},{3,2},{4,3},{5,4},{6,5},{7,6},{8,15},{9,8},{10,9... | collective-permute-start | bytes 147464 | tf_op jit(solution)/shard_map/ppermute | solution.py:55
  118.1 5.5 %collective-permute-start.4 = (bf16[24,1024]{1,0:T(8,128)(2,1)S(1)}, bf16[24,1024]{1,0:T(8,128)(2,1)S(1)}, u32[]{:S(2)}, u32[]{:S(2)}) collective-permute-start(bf16[24,1024]{1,0:T(8,128)(2,1)S(1)} %collective-permute-done.2), channel_id=1, source_target_pairs={{0,1},{1,2},{2,3},{3,4},{4,5},{5,6},{6,7},{7,0},{8,9},{9,10},{10,1... | collective-permute-start | bytes 147464 | tf_op jit(solution)/shard_map/ppermute | solution.py:50
  118.1 5.5 %collective-permute-start.5 = (bf16[24,1024]{1,0:T(8,128)(2,1)S(1)}, bf16[24,1024]{1,0:T(8,128)(2,1)S(1)}, u32[]{:S(2)}, u32[]{:S(2)}) collective-permute-start(bf16[24,1024]{1,0:T(8,128)(2,1)S(1)} %collective-permute-done.3), channel_id=1, source_target_pairs={{0,7},{1,0},{2,1},{3,2},{4,3},{5,4},{6,5},{7,6},{8,15},{9,8},{10,9... | collective-permute-start | bytes 147464 | tf_op jit(solution)/shard_map/ppermute | solution.py:55
  123.6 5.3 %collective-permute-start.6 = (bf16[24,1024]{1,0:T(8,128)(2,1)S(1)}, bf16[24,1024]{1,0:T(8,128)(2,1)S(1)}, u32[]{:S(2)}, u32[]{:S(2)}) collective-permute-start(bf16[24,1024]{1,0:T(8,128)(2,1)S(1)} %collective-permute-done.4), channel_id=1, source_target_pairs={{0,1},{1,2},{2,3},{3,4},{4,5},{5,6},{6,7},{7,0},{8,9},{9,10},{10,1... | collective-permute-start | bytes 147464 | tf_op jit(solution)/shard_map/ppermute | solution.py:50
  128.9 6.4 %copy-start = (bf16[192,1024]{1,0:T(8,128)(2,1)}, bf16[192,1024]{1,0:T(8,128)(2,1)S(1)}, u32[]{:S(2)}) copy-start(bf16[192,1024]{1,0:T(8,128)(2,1)S(1)} %constant_dynamic-update-slice_fusion.2) | copy-start | bytes 1179652
  135.3 99.8 %reduce-scatter.13.cloned.1.call-start = ((), (), s32[]{:S(2)}) async-start(), calls=%async_computation.11 | async-start | bytes 1769472 | tf_op jit(solution)/shard_map/reduce_scatter | solution.py:36
  145.2 113.4 %reduce-scatter.9.cloned.1.call-start = ((), (), s32[]{:S(2)}) async-start(), calls=%async_computation.8 | async-start | bytes 983040 | tf_op jit(solution)/shard_map/reduce_scatter | solution.py:68
  235.0 103.6 %reduce-scatter.15.cloned.1.call-start = ((), (), s32[]{:S(2)}) async-start(), calls=%async_computation.12 | async-start | bytes 1720320 | tf_op jit(solution)/shard_map/reduce_scatter | solution.py:83
  269.2 0.7 copy-start.3
  271.7 66.9 %copy-start.5 = (f32[48,3584]{1,0:T(8,128)S(1)}, f32[48,3584]{1,0:T(8,128)}, u32[]{:S(2)}) copy-start(f32[48,3584]{1,0:T(8,128)} %reduce-scatter.7.cloned.1.call-done) | copy-start | bytes 2064388
  306.7 33.8 %copy-start.4 = (bf16[192,1024]{1,0:T(8,128)(2,1)S(1)}, bf16[192,1024]{1,0:T(8,128)(2,1)}, u32[]{:S(2)}) copy-start(bf16[192,1024]{1,0:T(8,128)(2,1)} %copy-done.3) | copy-start | bytes 1179652
  311.3 58.6 %all-gather.5.cloned.1.call-start = ((), (), s32[]{:S(2)}) async-start(), calls=%async_computation.13 | async-start | bytes 1720320 | tf_op jit(solution)/shard_map/all_gather | solution.py:94
  340.5 67.5 %reduce-scatter.17.cloned.1.call-start = ((), (), s32[]{:S(2)}) async-start(), calls=%async_computation.14 | async-start | bytes 442368 | tf_op jit(solution)/shard_map/reduce_scatter | solution.py:98
  352.8 24.0 %copy-start.1 = (bf16[192,1024]{1,0:T(8,128)(2,1)S(1)}, bf16[192,1024]{1,0:T(8,128)(2,1)}, u32[]{:S(2)}) copy-start(bf16[192,1024]{1,0:T(8,128)(2,1)} %copy-done) | copy-start | bytes 1179652
  369.9 6.9 %copy-start.6 = (bf16[192,3584]{1,0:T(8,128)(2,1)S(1)}, bf16[192,3584]{1,0:T(8,128)(2,1)}, u32[]{:S(2)}) copy-start(bf16[192,3584]{1,0:T(8,128)(2,1)} %all-gather.5.cloned.1.call-done) | copy-start | bytes 4128772
Sparse Core Ops, SparseCore 0:
  39.1 64.6 reduce-scatter.10
  106.2 29.1 all-gather.2
  139.0 40.6 reduce-scatter.6
  182.4 36.0 reduce-scatter.12
  235.2 23.4 reduce-scatter.8
  311.4 27.1 reduce-scatter.14
  340.6 29.2 all-gather.4
  376.9 31.0 reduce-scatter.16
